TPU v7x, 256 devices: a whole 4x4x8 slice. The times are simulated.
256 devices in a mesh: mode: 16 (over x_hi, y, core), site: 16 (over z, x_lo).
Axes of the slice: x: 4 (x_hi: 2, x_lo: 2; x = x_hi * 2 + x_lo), y: 4, z: 8, core: 2. Of those that a mesh axis runs over, the one named last changes fastest.
Arguments:
- eigvecs: bfloat16 [2, 64, 3, 110592], P(None, 'mode', None, 'site'), may hold values from -6 to 6
- perams: bfloat16 [2, 16, 64, 64], replicated, may hold values from -0.75 to 0.75
- momenta: int32 [2, 3], replicated, may hold values from -2 to 2
- spins: int32 [16, 3], replicated, may hold values from 0 to 15
- pair_combs: int32 [16, 2], P('site'), may hold values from 0 to 15
- pair_moms: int32 [16, 2], P('site'), may hold values from 0 to 1
Outputs:
- exchange: float32 [16, 2, 64, 64], P('site', None, 'mode')
All inputs are finite; a program needn't handle non-finite values.
Results may differ from a plain program's by a relative error of at most 0.018.
Values may be sent and summed in bfloat16 or wider, within the bound.
No kernel may reach another device: no remote copies, remote signals or barrier semaphores. Data moves between devices by JAX's collectives and lax.ppermute only.
A program may use at most 64 MiB of HBM per device.

v0:
```python
import jax
import jax.numpy as jnp
from jax import lax
from jax.sharding import PartitionSpec as P

LAT = 48


def hartley(momenta, glob):
    coord_x = glob // (LAT * LAT)
    coord_y = glob // LAT % LAT
    coord_z = glob % LAT
    wave = (
        momenta[:, 0:1] * coord_x[None]
        + momenta[:, 1:2] * coord_y[None]
        + momenta[:, 2:3] * coord_z[None]
    ) % LAT
    theta = wave.astype(jnp.float32) * (2.0 * jnp.pi / LAT)
    return jnp.cos(theta) + jnp.sin(theta)


def body(eigvecs, perams, momenta, spins, pair_combs, pair_moms):
    nslice, mode_dev, _, site_dev = eigvecs.shape
    nmode = perams.shape[-1]
    nspin = perams.shape[1]
    ncomb = spins.shape[0]
    nmom = momenta.shape[0]
    comb_dev = ncomb // lax.axis_size("site")
    first_mode = lax.axis_index("mode") * mode_dev
    gathered = lax.all_gather(eigvecs, "mode", axis=1, tiled=True)
    glob = lax.axis_index("site") * site_dev + jnp.arange(site_dev, dtype=jnp.int32)
    phase = hartley(momenta, glob)

    def triplet_part(vectors):
        floats = vectors.astype(jnp.float32)
        own_modes = lax.dynamic_slice_in_dim(floats, first_mode, mode_dev, 0)
        left = own_modes[:, None]
        right = floats[None]
        cross_0 = left[:, :, 1] * right[:, :, 2] - left[:, :, 2] * right[:, :, 1]
        cross_1 = left[:, :, 2] * right[:, :, 0] - left[:, :, 0] * right[:, :, 2]
        cross_2 = left[:, :, 0] * right[:, :, 1] - left[:, :, 1] * right[:, :, 0]
        diquark = jnp.stack([cross_0, cross_1, cross_2], axis=2).astype(jnp.bfloat16)
        weighted = (phase[:, None, None, :] * floats[None]).astype(jnp.bfloat16)
        product = lax.dot_general(
            diquark.reshape(mode_dev * nmode, 3 * site_dev),
            weighted.reshape(nmom * nmode, 3 * site_dev),
            (((1,), (1,)), ((), ())),
            preferred_element_type=jnp.float32,
        )
        return product.reshape(mode_dev, nmode, nmom, nmode)

    partial_sums = lax.map(triplet_part, gathered)
    totals = lax.psum(partial_sums, "site")
    triplet = (totals * float(LAT) ** (-1.5)).astype(jnp.bfloat16)
    comb_ids = jnp.arange(ncomb, dtype=jnp.int32)
    mom_ids = jnp.arange(nmom, dtype=jnp.int32)
    spin_ids = jnp.arange(nspin, dtype=jnp.int32)
    own_spins = lax.dynamic_slice_in_dim(spins, lax.axis_index("site") * comb_dev, comb_dev, 0)
    picker = (own_spins[:, :, None] == spin_ids[None, None, :]).astype(jnp.bfloat16)
    chosen = jnp.einsum(
        "cks,tsmn->tckmn", picker, perams, preferred_element_type=jnp.float32
    ).astype(jnp.bfloat16)
    first = jnp.einsum(
        "tijpk,tcmk->tcijpm", triplet, chosen[:, :, 2], preferred_element_type=jnp.float32
    ).astype(jnp.bfloat16)
    second = jnp.einsum(
        "tcmj,tcijpk->itcpmk", chosen[:, :, 1], first, preferred_element_type=jnp.float32
    ).astype(jnp.bfloat16)
    rows_sel = chosen[:, :, 0]
    cols_sel = lax.dynamic_slice_in_dim(rows_sel, first_mode, mode_dev, 3)
    own_blocks = lax.psum_scatter(
        jnp.einsum("tcmi,itcpjk->mtcpjk", cols_sel, second, preferred_element_type=jnp.float32),
        "mode",
        scatter_dimension=0,
        tiled=True,
    ).astype(jnp.bfloat16)
    all_blocks = lax.all_gather(own_blocks, "site", axis=2, tiled=True)
    swapped = lax.all_to_all(all_blocks, "mode", split_axis=4, concat_axis=0, tiled=True)
    pick_left = (
        (pair_combs[:, 0][:, None, None] == comb_ids[None, :, None])
        & (pair_moms[:, 0][:, None, None] == mom_ids[None, None, :])
    ).astype(jnp.bfloat16)
    pick_right = (
        (pair_combs[:, 1][:, None, None] == comb_ids[None, :, None])
        & (pair_moms[:, 1][:, None, None] == mom_ids[None, None, :])
    ).astype(jnp.bfloat16)
    left_block = jnp.einsum(
        "qcp,itcpjk->qtijk", pick_left, all_blocks, preferred_element_type=jnp.float32
    ).astype(jnp.bfloat16)
    right_block = jnp.einsum(
        "qcp,mtcpnk->qtmnk", pick_right, swapped, preferred_element_type=jnp.float32
    ).astype(jnp.bfloat16)
    partial_corr = jnp.einsum(
        "qtijk,qtjil->qtkl", left_block, right_block, preferred_element_type=jnp.float32
    ) * (1.0 / nmode)
    return lax.psum_scatter(
        partial_corr.astype(jnp.bfloat16), "mode", scatter_dimension=2, tiled=True
    ).astype(jnp.float32)


def solution(mesh):
    placed = (P(None, "mode", None, "site"), P(), P(), P(), P("site", None), P("site", None))
    return jax.shard_map(
        body, mesh=mesh, in_specs=placed, out_specs=P("site", None, "mode", None), check_vma=False
    )
```

profile of v0, /device:TPU:38, one launch (start us, length us, event | category | flops | bytes accessed | tf_op | source)
XLA Modules:
  0.0 601.7 jit_solution(13482562929319963017)
XLA Ops:
  6.5 0.0 copy-start
  6.5 0.0 all-gather.3.cloned.1.call-start
  6.5 2.0 copy.22
  8.6 0.0 all-gather.3.cloned.1.call-update
  8.6 0.0 all-reduce.3.cloned.1.call-start
  8.7 0.9 dynamic-slice_reduce_fusion
  9.5 1.0 slice_reduce_fusion
  10.6 0.1 add_select_fusion
  10.6 0.4 fusion.23
  11.1 64.4 %all-gather.3.cloned.1.call-done = bf16[2,64,3,6912]{3,0,2,1:T(2,128)(2,1)} async-done(((bf16[2,4,3,6912]{3,0,2,1:T(2,128)(2,1)}), bf16[2,64,3,6912]{3,0,2,1:T(2,128)(2,1)}) %all-gather.3.cloned.1.call-update) | async-done | bytes 5308432 | tf_op jit(solution)/shard_map/all_gather | solution.py:30
  75.5 5.4 copy.23
  80.9 20.2 %while.13 = (s32[]{:T(128)}, f32[2,4,64,2,64]{4,2,3,1,0:T(8,128)S(1)}, bf16[2,64,3,6912]{3,1,2,0:T(8,128)(2,1)}, s32[]{:T(128)}, s32[6912]{0:T(1024)S(1)}, /*ind...) while((s32[]{:T(128)}, ...), condition=%wide.region_1.2_spmd.clone, body=%wide.region_0.1_spmd.clone.sunk | while | flops 1418867712 | bytes 57853072 | solution.py:52
  80.9 2.4 dynamic-slice_convert_fusion.3
  83.3 0.1 dynamic-slice_bitcast_fusion.2
  83.4 0.3 slice_bitcast_fusion.8
  83.8 3.2 subtract_convert_fusion.4
  86.9 1.0 sine_add_fusion.2
  88.0 3.0 fusion.62
  91.0 2.4 dynamic-slice_convert_fusion.3
  93.4 0.1 dynamic-slice_bitcast_fusion.2
  93.5 0.3 slice_bitcast_fusion.8
  93.9 3.2 subtract_convert_fusion.4
  97.0 1.0 sine_add_fusion.2
  98.1 3.0 fusion.62
  101.1 0.0 copy-start.2
  101.1 0.8 copy-done.2
  101.9 0.0 all-reduce.3.cloned.1.call-update
  101.9 0.0 reduce-scatter.3.cloned.1.call-start
  101.9 0.1 fusion.54
  102.1 0.1 constant_dynamic-slice_fusion
  102.2 0.1 copy.24
  102.3 135.7 %all-reduce.3.cloned.1.call-done = f32[2,4,64,2,64]{4,2,3,1,0:T(8,128)} async-done(((f32[2,4,64,2,64]{4,2,3,1,0:T(8,128)}), f32[2,4,64,2,64]{4,2,3,1,0:T(8,128)}) %all-reduce.3.cloned.1.call-update) | async-done | bytes 262160 | tf_op jit(solution)/shard_map/psum | solution.py:53
  238.1 1.6 fusion.22
  239.6 0.2 copy.25
  239.8 4.9 convolution_bitcast_fusion
  244.8 9.1 %copy.26 = f32[64,2,1,2,64,64]{5,4,3,2,1,0:T(8,128)} copy(f32[64,2,1,2,64,64]{0,5,4,3,1,2:T(8,128)} %convolution_bitcast_fusion) | data formatting | bytes 8388608 | tf_op jit(solution)/shard_map/tcmi,itcpjk->mtcpjk/transpose | solution.py:72
  253.9 0.0 reduce-scatter.3.cloned.1.call-update
  253.9 0.2 all-gather.5.cloned.1.call-start
  254.1 109.6 %reduce-scatter.3.cloned.1.call-done = f32[4,2,1,2,64,64]{5,4,3,2,1,0:T(8,128)} async-done(((f32[64,2,1,2,64,64]{5,4,3,2,1,0:T(8,128)}), f32[4,2,1,2,64,64]{5,4,3,2,1,0:T(8,128)}) %reduce-scatter.3.cloned.1.call-update) | async-done | bytes 262160 | tf_op jit(solution)/shard_map/reduce_scatter | solution.py:71
  363.7 1.8 convert_bitcast_fusion
  365.5 0.0 all-gather.5.cloned.1.call-update
  365.5 99.9 %all-gather.5.cloned.1.call-done = bf16[4,2,16,2,64,64]{5,4,3,1,0,2:T(8,128)(2,1)} async-done(((bf16[4,2,1,2,64,64]{5,4,3,1,0,2:T(8,128)(2,1)}), bf16[4,2,16,2,64,64]{5,4,3,1,0,2:T(8,128)(2,1)}) %all-gather.5.cloned.1.call-update) | async-done | bytes 2097168 | tf_op jit(solution)/shard_map/all_gather | solution.py:77
  465.4 6.9 %copy.74 = bf16[4,2,16,2,64,64]{5,2,3,1,0,4:T(8,128)(2,1)} copy(bf16[4,2,16,2,64,64]{5,4,3,1,0,2:T(8,128)(2,1)} %all-gather.5.cloned.1.call-done) | data formatting | bytes 4194304 | tf_op jit(solution)/shard_map/all_gather | solution.py:77
  472.3 7.6 %reshape.298 = bf16[16,2,32768]{2,1,0:T(2,128)(2,1)} reshape(bf16[64,4,2,2,16,64]{5,4,3,2,1,0:T(8,128)(2,1)} %bitcast.161) | data formatting | bytes 4194304
  479.9 7.3 %all-to-all-start = ((bf16[16,2,32768]{2,1,0:T(2,128)(2,1)}), bf16[16,2,32768]{2,1,0:T(2,128)(2,1)S(1)}, u32[]{:S(2)}, u32[]{:S(2)}) async-start(bf16[16,2,32768]{2,1,0:T(2,128)(2,1)} %reshape.298), calls=%async_computation.1 | async-start | bytes 4194304 | tf_op jit(solution)/shard_map/all_to_all | solution.py:78
  487.2 0.6 dynamic-slice.2
  488.4 0.6 fusion.56
  489.0 0.6 iota_compare_fusion.1
  489.6 0.0 copy-done.4
  489.7 0.6 fusion.55
  490.3 0.6 iota_compare_fusion.2
  490.9 0.6 iota_compare_fusion.3
  491.5 0.7 iota_compare_fusion.4
  492.2 0.1 and_bitcast_fusion
  492.2 0.1 and_convert_fusion
  492.3 3.4 multiply_reduce_fusion
  495.7 0.1 copy.43
  495.8 18.6 %all-to-all-done = bf16[16,2,32768]{2,1,0:T(2,128)(2,1)S(1)} async-done(((bf16[16,2,32768]{2,1,0:T(2,128)(2,1)}), bf16[16,2,32768]{2,1,0:T(2,128)(2,1)S(1)}, u32[]{:S(2)}, u32[]{:S(2)}) %all-to-all-start) | async-done | bytes 2097184 | tf_op jit(solution)/shard_map/all_to_all | solution.py:78
  514.4 5.0 reshape.299
  519.4 3.4 copy.30
  522.8 0.7 convolution_bitcast_fusion.1
  523.5 0.2 fusion.26
  523.8 70.8 %all-reduce = bf16[1,2,64,64]{3,2,1,0:T(8,128)(2,1)S(1)} all-reduce(bf16[1,2,64,64]{3,2,1,0:T(8,128)(2,1)S(1)} %fusion.26), channel_id=3, replica_groups=mesh['mode'=16,'site'=16] {'mode'}, use_global_device_ids=true, to_apply=%region_4.5.clone | all-reduce | flops 8192 | bytes 32768
  594.5 0.6 dynamic-slice_convert_fusion.1
  (12 shorter events, 0.1 us)
Async XLA Ops:
  6.5 4.1 copy-start
  6.5 68.9 %all-gather.3.cloned.1.call-start = ((), (), s32[]{:S(2)}) async-start(), calls=%async_computation.2 | async-start | bytes 5640192 | tf_op jit(solution)/shard_map/all_gather | solution.py:30
  8.6 229.5 %all-reduce.3.cloned.1.call-start = ((), (), s32[]{:S(2)}) async-start(), calls=%async_computation.3 | async-start | bytes 1048576 | tf_op jit(solution)/shard_map/psum | solution.py:53
  101.1 0.8 copy-start.2
  101.9 261.8 %reduce-scatter.3.cloned.1.call-start = ((), (), s32[]{:S(2)}) async-start(), calls=%async_computation.4 | async-start | bytes 8912896 | tf_op jit(solution)/shard_map/reduce_scatter | solution.py:71
  253.9 211.5 %all-gather.5.cloned.1.call-start = ((), (), s32[]{:S(2)}) async-start(), calls=%async_computation.5 | async-start | bytes 4456448 | tf_op jit(solution)/shard_map/all_gather | solution.py:77
  472.3 14.9 %copy-start.5 = (u32[256]{0:T(256)S(1)}, u32[256]{0:T(256)}, u32[]{:S(2)}) copy-start(u32[256]{0:T(256)} %constant.88) | copy-start | bytes 3076
  472.3 16.1 %copy-start.3 = (s32[1,2]{1,0:T(1,128)S(1)}, s32[1,2]{1,0:T(1,128)}, u32[]{:S(2)}) copy-start(s32[1,2]{1,0:T(1,128)} %param.13) | copy-start | bytes 28
  472.3 17.3 %copy-start.4 = (s32[1,2]{1,0:T(1,128)S(1)}, s32[1,2]{1,0:T(1,128)}, u32[]{:S(2)}) copy-start(s32[1,2]{1,0:T(1,128)} %param.12) | copy-start | bytes 28
  479.9 34.5 %all-to-all-start = ((bf16[16,2,32768]{2,1,0:T(2,128)(2,1)}), bf16[16,2,32768]{2,1,0:T(2,128)(2,1)S(1)}, u32[]{:S(2)}, u32[]{:S(2)}) async-start(bf16[16,2,32768]{2,1,0:T(2,128)(2,1)} %reshape.298), calls=%async_computation.1 | async-start | bytes 4194304 | tf_op jit(solution)/shard_map/all_to_all | solution.py:78
  519.4 75.7 %copy-start.1 = (bf16[2,16,64,64]{3,2,1,0:T(8,128)(2,1)S(1)}, bf16[2,16,64,64]{3,2,1,0:T(8,128)(2,1)}, u32[]{:S(2)}) copy-start(bf16[2,16,64,64]{3,2,1,0:T(8,128)(2,1)} %param.9) | copy-start | bytes 786436
Sparse Core Ops, SparseCore 0:
  10.0 65.4 all-gather.2
  102.0 136.0 all-reduce.2
  254.0 109.6 reduce-scatter.2
  365.6 99.7 all-gather.4
where the time goes:
time: 602 us
  waiting for transfers between devices  428 us (71%)
  blocking collectives  70.8 us (12%)
  local copies, waits for them, and re-layouts  45.4 us (8%)
  other arithmetic  21.7 us (4%)
  between operations  13.9 us (2%)
  matrix products  13.8 us (2%)
  starting transfers between devices  7.58 us (1%)
    psum x1, waiting for transfers between devices, body(): totals = lax.psum(partial_sums, 'site')  136 us
    reduce_scatter x1, waiting for transfers between devices, body(): lax.psum_scatter(jnp.einsum('tcmi,itcpjk->mtcpjk', cols_sel, second, pref...  110 us
    all_gather x1, waiting for transfers between devices, body(): all_blocks = lax.all_gather(own_blocks, 'site', axis=2, tiled=True)  99.9 us
    unnamed x1, blocking collectives  70.8 us
    all_gather x1, waiting for transfers between devices, body(): gathered = lax.all_gather(eigvecs, 'mode', axis=1, tiled=True)  64.4 us
    unnamed x17, local copies, waits for them, and re-layouts  21.4 us
    all_to_all x1, waiting for transfers between devices, body(): lax.all_to_all(all_blocks, 'mode', split_axis=4, concat_axis=0, tiled=True)  18.6 us
  transfers between devices with their start and end apart: 5, of which 5 were waited for; matrix products, arithmetic and copies ran while one was open for 2% of the time, Pallas kernels for 0%

commit v1 on v0

--- a/solution.py
+++ b/solution.py
@@ -74,7 +74,10 @@
         scatter_dimension=0,
         tiled=True,
     ).astype(jnp.bfloat16)
-    all_blocks = lax.all_gather(own_blocks, "site", axis=2, tiled=True)
+    size = lax.axis_size("site")
+    tiles = jnp.stack([own_blocks for _ in range(size)])
+    tiles = lax.all_to_all(tiles, "site", split_axis=0, concat_axis=0)
+    all_blocks = jnp.concatenate(tiles, axis=2)
     swapped = lax.all_to_all(all_blocks, "mode", split_axis=4, concat_axis=0, tiled=True)
     pick_left = (
         (pair_combs[:, 0][:, None, None] == comb_ids[None, :, None])

time: 602 us -> 577 us (0.958)
  waiting for transfers between devices: 428 us -> 327 us
  blocking collectives: 70.8 us -> 126 us
  local copies, waits for them, and re-layouts: 45.4 us -> 64.9 us
    all_gather x1 -> x0, waiting for transfers between devices: 99.9 us -> none  [body(): all_blocks = lax.all_gather(own_blocks, 'site', axis=2, tiled=True)]
    all_to_all x0 -> x1, blocking collectives: none -> 55 us  [body(): tiles = lax.all_to_all(tiles, 'site', split_axis=0, concat_axis=0)]
    unnamed x17 -> x22, local copies, waits for them, and re-layouts: 21.4 us -> 40 us
    reshape x0 -> x2, local copies, waits for them, and re-layouts: none -> 7.83 us  [body(): all_blocks = jnp.concatenate(tiles, axis=2)]
    all_gather x1 -> x0, local copies, waits for them, and re-layouts: 6.86 us -> none  [body(): all_blocks = lax.all_gather(own_blocks, 'site', axis=2, tiled=True)]
  transfers between devices with their start and end apart: 5 -> 4, of which waited for: 5 -> 4; matrix products, arithmetic and copies ran while one was open for 2% -> 2% of each run, Pallas kernels for 0% -> 0%
where the time goes in v1:
time: 577 us; the launch traced here: 575 us
  waiting for transfers between devices  327 us (57%)
  blocking collectives  126 us (22%)
  local copies, waits for them, and re-layouts  64.9 us (11%)
  matrix products  18.5 us (3%)
  other arithmetic  17.7 us (3%)
  between operations  13.9 us (2%)
  starting transfers between devices  6.72 us (1%)
    psum x1, waiting for transfers between devices, body(): totals = lax.psum(partial_sums, 'site')  136 us
    reduce_scatter x1, waiting for transfers between devices, body(): lax.psum_scatter(jnp.einsum('tcmi,itcpjk->mtcpjk', cols_sel, second, pref...  110 us
    unnamed x1, blocking collectives  70.8 us
    all_gather x1, waiting for transfers between devices, body(): gathered = lax.all_gather(eigvecs, 'mode', axis=1, tiled=True)  64.4 us
    all_to_all x1, blocking collectives, body(): tiles = lax.all_to_all(tiles, 'site', split_axis=0, concat_axis=0)  55 us
    unnamed x22, local copies, waits for them, and re-layouts  40 us
    all_to_all x1, waiting for transfers between devices, body(): lax.all_to_all(all_blocks, 'mode', split_axis=4, concat_axis=0, tiled=True)  17.3 us
  transfers between devices with their start and end apart: 4, of which 4 were waited for; matrix products, arithmetic and copies ran while one was open for 2% of the time, Pallas kernels for 0%

profile of v1, /device:TPU:38, one launch (start us, length us, event | category | flops | bytes accessed | tf_op | source)
XLA Modules:
  0.0 574.8 jit_solution(16845803131576096457)
XLA Ops:
  6.5 0.0 all-gather.2.cloned.1.call-start
  6.5 2.0 copy.20
  8.6 0.0 all-gather.2.cloned.1.call-update
  8.6 0.0 all-reduce.3.cloned.1.call-start
  8.7 0.9 dynamic-slice_reduce_fusion
  9.5 1.0 slice_reduce_fusion
  10.6 0.1 add_select_fusion
  10.6 0.4 fusion.25
  11.0 64.4 %all-gather.2.cloned.1.call-done = bf16[2,64,3,6912]{3,0,2,1:T(2,128)(2,1)} async-done(((bf16[2,4,3,6912]{3,0,2,1:T(2,128)(2,1)}), bf16[2,64,3,6912]{3,0,2,1:T(2,128)(2,1)}) %all-gather.2.cloned.1.call-update) | async-done | bytes 5308432 | tf_op jit(solution)/shard_map/all_gather | solution.py:30
  75.5 5.4 copy.21
  80.9 20.2 %while.13 = (s32[]{:T(128)}, f32[2,4,64,2,64]{4,2,3,1,0:T(8,128)S(1)}, bf16[2,64,3,6912]{3,1,2,0:T(8,128)(2,1)}, s32[]{:T(128)}, s32[6912]{0:T(1024)S(1)}, /*ind...) while((s32[]{:T(128)}, ...), condition=%wide.region_1.2_spmd.clone, body=%wide.region_0.1_spmd.clone.sunk | while | flops 1418867712 | bytes 57853072 | solution.py:52
  80.9 2.4 dynamic-slice_convert_fusion.3
  83.3 0.1 dynamic-slice_bitcast_fusion.2
  83.4 0.3 slice_bitcast_fusion.8
  83.8 3.2 subtract_convert_fusion.4
  86.9 1.0 sine_add_fusion.2
  88.0 3.0 fusion.65
  91.0 2.4 dynamic-slice_convert_fusion.3
  93.4 0.1 dynamic-slice_bitcast_fusion.2
  93.5 0.3 slice_bitcast_fusion.8
  93.9 3.2 subtract_convert_fusion.4
  97.0 1.0 sine_add_fusion.2
  98.1 3.0 fusion.65
  101.1 0.8 copy-done.3
  101.9 0.0 all-reduce.3.cloned.1.call-update
  101.9 0.0 reduce-scatter.3.cloned.1.call-start
  101.9 0.1 fusion.57
  102.1 0.1 constant_dynamic-slice_fusion
  102.2 0.1 copy.22
  102.3 135.5 %all-reduce.3.cloned.1.call-done = f32[2,4,64,2,64]{4,2,3,1,0:T(8,128)} async-done(((f32[2,4,64,2,64]{4,2,3,1,0:T(8,128)}), f32[2,4,64,2,64]{4,2,3,1,0:T(8,128)}) %all-reduce.3.cloned.1.call-update) | async-done | bytes 262160 | tf_op jit(solution)/shard_map/psum | solution.py:53
  237.8 1.6 fusion.24
  239.4 0.2 copy.23
  239.6 4.9 convolution_bitcast_fusion
  244.6 9.1 %copy.24 = f32[64,2,1,2,64,64]{5,4,3,2,1,0:T(8,128)} copy(f32[64,2,1,2,64,64]{0,5,4,3,1,2:T(8,128)} %convolution_bitcast_fusion) | data formatting | bytes 8388608 | tf_op jit(solution)/shard_map/tcmi,itcpjk->mtcpjk/transpose | solution.py:72
  253.6 0.0 reduce-scatter.3.cloned.1.call-update
  253.7 109.8 %reduce-scatter.3.cloned.1.call-done = f32[4,2,1,2,64,64]{5,4,3,2,1,0:T(8,128)} async-done(((f32[64,2,1,2,64,64]{5,4,3,2,1,0:T(8,128)}), f32[4,2,1,2,64,64]{5,4,3,2,1,0:T(8,128)}) %reduce-scatter.3.cloned.1.call-update) | async-done | bytes 262160 | tf_op jit(solution)/shard_map/reduce_scatter | solution.py:71
  363.5 1.1 convert_bitcast_fusion
  364.5 3.0 broadcast_bitcast_fusion
  367.5 6.3 %reshape.352 = bf16[16,2,32768]{2,1,0:T(2,128)(2,1)S(1)} reshape(bf16[16,1,4,2,2,64,64]{6,5,4,3,2,1,0:T(8,128)(2,1)} %broadcast_bitcast_fusion) | data formatting | bytes 4194304
  373.9 55.0 %all_to_all.23 = bf16[16,2,32768]{2,1,0:T(2,128)(2,1)} all-to-all(bf16[16,2,32768]{2,1,0:T(2,128)(2,1)S(1)} %reshape.352), channel_id=1, replica_groups=mesh['mode'=16,'site'=16] {'site'}, dimensions={0} | all-to-all | bytes 4194304 | tf_op jit(solution)/shard_map/all_to_all | solution.py:79
  428.9 7.4 %reshape.353 = bf16[16,1,4,2,2,64,64]{6,5,4,3,2,1,0:T(8,128)(2,1)} reshape(bf16[16,2,32768]{2,1,0:T(2,128)(2,1)} %all_to_all.23) | data formatting | bytes 4194304
  436.3 3.1 bitcast_bitcast_fusion
  439.5 1.9 copy-done.2
  441.4 4.7 copy.70
  446.1 7.6 %reshape.354 = bf16[16,2,32768]{2,1,0:T(2,128)(2,1)} reshape(bf16[64,4,2,2,16,64]{5,4,3,2,1,0:T(8,128)(2,1)} %bitcast.176) | data formatting | bytes 4194304
  453.6 6.6 %all-to-all-start.1 = ((bf16[16,2,32768]{2,1,0:T(2,128)(2,1)}), bf16[16,2,32768]{2,1,0:T(2,128)(2,1)S(1)}, u32[]{:S(2)}, u32[]{:S(2)}) async-start(bf16[16,2,32768]{2,1,0:T(2,128)(2,1)} %reshape.354), calls=%async_computation.2 | async-start | bytes 4194304 | tf_op jit(solution)/shard_map/all_to_all | solution.py:81
  460.3 0.6 dynamic-slice.2
  461.5 0.6 fusion.58
  462.1 0.6 iota_compare_fusion.1
  462.8 0.6 fusion.59
  463.4 0.6 iota_compare_fusion.2
  464.0 0.6 iota_compare_fusion.3
  464.7 0.6 iota_compare_fusion.4
  465.3 0.1 and_bitcast_fusion
  465.3 0.1 and_bitcast_fusion.1
  465.4 4.6 fusion.21
  470.0 0.1 copy.36
  470.2 17.3 %all-to-all-done.1 = bf16[16,2,32768]{2,1,0:T(2,128)(2,1)S(1)} async-done(((bf16[16,2,32768]{2,1,0:T(2,128)(2,1)}), bf16[16,2,32768]{2,1,0:T(2,128)(2,1)S(1)}, u32[]{:S(2)}, u32[]{:S(2)}) %all-to-all-start.1) | async-done | bytes 2097184 | tf_op jit(solution)/shard_map/all_to_all | solution.py:81
  487.5 5.0 reshape.355
  492.5 3.4 copy.27
  495.9 0.7 convolution_bitcast_fusion.1
  496.6 0.2 fusion.28
  496.9 70.8 %all-reduce = bf16[1,2,64,64]{3,2,1,0:T(8,128)(2,1)S(1)} all-reduce(bf16[1,2,64,64]{3,2,1,0:T(8,128)(2,1)S(1)} %fusion.28), channel_id=3, replica_groups=mesh['mode'=16,'site'=16] {'mode'}, use_global_device_ids=true, to_apply=%region_4.5.clone | all-reduce | flops 8192 | bytes 32768
  567.6 0.6 dynamic-slice_convert_fusion.1
  (16 shorter events, 0.1 us)
Async XLA Ops:
  6.5 4.1 copy-start
  6.5 68.9 %all-gather.2.cloned.1.call-start = ((), (), s32[]{:S(2)}) async-start(), calls=%async_computation.3 | async-start | bytes 5640192 | tf_op jit(solution)/shard_map/all_gather | solution.py:30
  8.6 229.3 %all-reduce.3.cloned.1.call-start = ((), (), s32[]{:S(2)}) async-start(), calls=%async_computation.4 | async-start | bytes 1048576 | tf_op jit(solution)/shard_map/psum | solution.py:53
  101.1 0.8 copy-start.3
  101.9 261.6 %reduce-scatter.3.cloned.1.call-start = ((), (), s32[]{:S(2)}) async-start(), calls=%async_computation.5 | async-start | bytes 8912896 | tf_op jit(solution)/shard_map/reduce_scatter | solution.py:71
  439.4 1.9 copy-start.2
  446.1 14.2 %copy-start.6 = (u32[256]{0:T(256)S(1)}, u32[256]{0:T(256)}, u32[]{:S(2)}) copy-start(u32[256]{0:T(256)} %constant.87) | copy-start | bytes 3076
  446.1 15.4 %copy-start.4 = (s32[1,2]{1,0:T(1,128)S(1)}, s32[1,2]{1,0:T(1,128)}, u32[]{:S(2)}) copy-start(s32[1,2]{1,0:T(1,128)} %param.13) | copy-start | bytes 28
  446.1 16.7 %copy-start.5 = (s32[1,2]{1,0:T(1,128)S(1)}, s32[1,2]{1,0:T(1,128)}, u32[]{:S(2)}) copy-start(s32[1,2]{1,0:T(1,128)} %param.12) | copy-start | bytes 28
  453.6 33.9 %all-to-all-start.1 = ((bf16[16,2,32768]{2,1,0:T(2,128)(2,1)}), bf16[16,2,32768]{2,1,0:T(2,128)(2,1)S(1)}, u32[]{:S(2)}, u32[]{:S(2)}) async-start(bf16[16,2,32768]{2,1,0:T(2,128)(2,1)} %reshape.354), calls=%async_computation.2 | async-start | bytes 4194304 | tf_op jit(solution)/shard_map/all_to_all | solution.py:81
  492.5 75.7 %copy-start.1 = (bf16[2,16,64,64]{3,2,1,0:T(8,128)(2,1)S(1)}, bf16[2,16,64,64]{3,2,1,0:T(8,128)(2,1)}, u32[]{:S(2)}) copy-start(bf16[2,16,64,64]{3,2,1,0:T(8,128)(2,1)} %param.9) | copy-start | bytes 786436
Sparse Core Ops, SparseCore 0:
  10.0 65.4 all-gather.1
  102.0 135.8 all-reduce.2
  253.8 109.6 reduce-scatter.2
